TPU v7x, 256 devices: a whole 4x4x8 slice. The times are simulated.
256 devices in a mesh: region: 32 (over x, z), group: 8 (over y, core).
Axes of the slice: x: 4, y: 4, z: 8, core: 2. Of those that a mesh axis runs over, the one named last changes fastest.
Arguments:
- block_coords: int32 [8, 192, 3], P('group', 'region'), may hold values from -100 to 63, as said below
- features: bfloat16 [8, 192, 8, 8, 8, 128], P('group', 'region'), may hold values from -6 to 6
- cotangent: bfloat16 [8, 192, 4, 4, 4, 128], P('group', 'region'), may hold values from -6 to 6
- weights: bfloat16 [3, 3, 3, 128, 128], replicated, may hold values from -0.109375 to 0.109375
Outputs:
- coarse_features: bfloat16 [8, 192, 4, 4, 4, 128], P('group', 'region')
- grad_features: bfloat16 [8, 192, 8, 8, 8, 128], P('group', 'region')
- grad_weight: float32 [3, 3, 3, 128, 128], replicated
Inputs may be any that keep to these rules, and one draw needn't show every extreme that they name: `block_coords`: slot s of device r along region holds a block with coordinates (x, y, z), x being 2r or 2r+1, 0 <= y < 1, 0 <= z < 4; a device's blocks are distinct; its occupied slots come first and the others hold -100 in all three coordinates; every device holds 3 to 6 blocks, and in each map one device holds 6 and another 6 // 2.
All inputs are finite; a program needn't handle non-finite values.
Results may differ from a plain program's by a relative error of at most 0.0023.
Values may be sent and summed in bfloat16 or wider, within the bound.
No kernel may reach another device: no remote copies, remote signals or barrier semaphores. Data moves between devices by JAX's collectives and lax.ppermute only.
A program may use at most 64 MiB of HBM per device.

v0:
```python
import math
import jax
import jax.numpy as jnp
from jax import lax
from jax.sharding import PartitionSpec as P

CROSS_Y = 1
CROSS_Z = 4
LOWER_SIDES = (
    (-1, 0, 0),
    (-1, -1, 0),
    (-1, 0, -1),
    (-1, -1, -1),
    (0, -1, 0),
    (0, 0, -1),
    (0, -1, -1),
)


def shifted(block, axis, distance):
    devices = range(lax.axis_size(axis))
    route = [(i - distance, i) for i in devices if i - distance in devices]
    return lax.ppermute(block, axis, route)


def unfold(volume, which_axis):
    pieces = [lax.slice_in_dim(volume, offset, offset + 7, 2, which_axis) for offset in range(3)]
    return jnp.stack(pieces, axis=which_axis + 1)


def fold_back(col_terms, which_axis):
    lower_part, middle_part, upper_part = [
        lax.index_in_dim(col_terms, offset, which_axis + 1, keepdims=False) for offset in range(3)
    ]
    zero_row = jnp.zeros_like(lax.slice_in_dim(lower_part, 0, 1, 1, which_axis))
    even_rows = jnp.concatenate([lower_part, zero_row], which_axis) + jnp.concatenate(
        [zero_row, upper_part], which_axis
    )
    paired = jnp.stack(
        [lax.slice_in_dim(even_rows, 0, 4, 1, which_axis), middle_part], which_axis + 1
    )
    new_shape = list(lower_part.shape)
    new_shape[which_axis] = 8
    merged = paired.reshape(new_shape)
    return jnp.concatenate([merged, lax.slice_in_dim(even_rows, 4, 5, 1, which_axis)], which_axis)


def pick_rows(lookup_table, link):
    safe_rows = jnp.clip(link[0], 0, lookup_table.shape[0] - 1)
    gathered = jnp.take(lookup_table, safe_rows, axis=0)
    present_mask = link[1].reshape((-1,) + (1,) * (gathered.ndim - 1))
    return jnp.where(present_mask, gathered, jnp.zeros_like(gathered))


def assemble(blocks, planes, source_links):
    face_x = pick_rows(planes, source_links[0])
    edge_xy = pick_rows(planes[:, 7], source_links[1])
    edge_xz = pick_rows(planes[:, :, 7], source_links[2])
    corner = pick_rows(planes[:, 7, 7], source_links[3])
    face_y = pick_rows(blocks[:, :, 7], source_links[4])
    face_z = pick_rows(blocks[:, :, :, 7], source_links[5])
    edge_yz = pick_rows(blocks[:, :, 7, 7], source_links[6])
    first_plane = jnp.concatenate(
        [
            jnp.concatenate([corner[:, None, None], edge_xy[:, None]], axis=2),
            jnp.concatenate([edge_xz[:, :, None], face_x], axis=2),
        ],
        axis=1,
    )
    low_row = jnp.concatenate([edge_yz[:, :, None], face_y], axis=2)[:, :, None]
    interior = jnp.concatenate([face_z[:, :, :, None], blocks], axis=3)
    upper_part = jnp.concatenate([low_row, interior], axis=2)
    return jnp.concatenate([first_plane[:, None], upper_part], axis=1)


def aim_rows(link, limit):
    return jnp.where(link[1], link[0], limit)


def spread_rims(ext_grads, source_links, block_count, table_rows):
    own_grad = ext_grads[:, 1:, 1:, 1:]
    planes = jnp.zeros((table_rows,) + own_grad.shape[2:], ext_grads.dtype)
    planes = planes.at[aim_rows(source_links[0], table_rows)].add(
        ext_grads[:, 0, 1:, 1:], mode="drop"
    )
    planes = planes.at[aim_rows(source_links[1], table_rows), 7].add(
        ext_grads[:, 0, 0, 1:], mode="drop"
    )
    planes = planes.at[aim_rows(source_links[2], table_rows), :, 7].add(
        ext_grads[:, 0, 1:, 0], mode="drop"
    )
    planes = planes.at[aim_rows(source_links[3], table_rows), 7, 7].add(
        ext_grads[:, 0, 0, 0], mode="drop"
    )
    own_grad = own_grad.at[aim_rows(source_links[4], block_count), :, 7].add(
        ext_grads[:, 1:, 0, 1:], mode="drop"
    )
    own_grad = own_grad.at[aim_rows(source_links[5], block_count), :, :, 7].add(
        ext_grads[:, 1:, 1:, 0], mode="drop"
    )
    own_grad = own_grad.at[aim_rows(source_links[6], block_count), :, 7, 7].add(
        ext_grads[:, 1:, 0, 0], mode="drop"
    )
    return (own_grad, planes)


def find_links(coords, region_rank, block_count):
    slot_ids = jnp.arange(block_count, dtype=jnp.int32)
    collected = []
    for side in LOWER_SIDES:
        wanted = coords + jnp.array(side, jnp.int32)
        matches = jnp.all(wanted[:, None, :] == coords[None, :, :], axis=2)
        present = jnp.any(matches, axis=1)
        source = jnp.sum(jnp.where(matches, slot_ids[None, :], 0), axis=1)
        if side[0] == -1:
            remote = (
                (wanted[:, 0] == 2 * region_rank - 1)
                & (wanted[:, 1] >= 0)
                & (wanted[:, 1] < CROSS_Y)
                & (wanted[:, 2] >= 0)
                & (wanted[:, 2] < CROSS_Z)
            )
            source = jnp.where(present, source, block_count + wanted[:, 1] * CROSS_Z + wanted[:, 2])
            present = present | remote
        collected.append((source, present))
    return collected


def per_device(block_coords, features, cotangent, weights):
    coords = block_coords[0]
    blocks = features[0]
    upstream = cotangent[0]
    block_count = blocks.shape[0]
    cell_count = CROSS_Y * CROSS_Z
    region_rank = lax.axis_index("region")
    occupied = coords[:, 0] >= 0
    cell_index = coords[:, 1] * CROSS_Z + coords[:, 2]
    in_top = coords[:, 0] == 2 * region_rank + 1
    top_planes = blocks[:, 7]
    outgoing = (
        jnp.zeros((cell_count,) + top_planes.shape[1:], blocks.dtype)
        .at[jnp.where(in_top, cell_index, cell_count)]
        .set(top_planes, mode="drop")
    )
    incoming = shifted(outgoing, "region", 1)
    source_links = find_links(coords, region_rank, block_count)
    plane_table = jnp.concatenate([top_planes, incoming], axis=0)
    extended = assemble(blocks, plane_table, source_links)
    columns = unfold(unfold(unfold(extended, 1), 3), 5)
    block_mask = occupied[:, None, None, None, None]
    result = jnp.einsum(
        "nxaybzcf,abcfo->nxyzo", columns, weights, preferred_element_type=jnp.float32
    )
    coarse = jnp.where(block_mask, result, 0.0).astype(jnp.bfloat16)
    masked = jnp.where(block_mask, upstream, jnp.zeros_like(upstream))
    local_grad = jnp.einsum(
        "nxaybzcf,nxyzo->abcfo", columns, masked, preferred_element_type=jnp.float32
    )
    col_terms = jnp.einsum(
        "nxyzo,abcfo->nxaybzcf", masked, weights, preferred_element_type=jnp.float32
    )
    ext_grads = fold_back(fold_back(fold_back(col_terms, 5), 3), 1)
    own_grad, plane_grads = spread_rims(
        ext_grads, source_links, block_count, block_count + cell_count
    )
    own_grad = own_grad.at[:, 7].add(plane_grads[:block_count])
    returned = shifted(plane_grads[block_count:].astype(jnp.bfloat16), "region", -1).astype(
        jnp.float32
    )
    own_grad = own_grad.at[:, 7].add(pick_rows(returned, (cell_index, in_top)))
    summed = lax.psum(local_grad, ("region", "group"))
    grad_scale = 1.0 / math.sqrt(
        lax.axis_size("group") * lax.axis_size("region") * block_count * upstream.shape[1] ** 3
    )
    return (coarse[None], own_grad.astype(jnp.bfloat16)[None], summed * grad_scale)


def solution(mesh):
    return jax.shard_map(
        per_device,
        mesh=mesh,
        in_specs=(
            P("group", "region", None),
            P("group", "region", None, None, None, None),
            P("group", "region", None, None, None, None),
            P(),
        ),
        out_specs=(
            P("group", "region", None, None, None, None),
            P("group", "region", None, None, None, None),
            P(),
        ),
        check_vma=False,
    )
```

profile of v0, /device:TPU:2, one launch (start us, length us, event | category | flops | bytes accessed | tf_op | source)
XLA Modules:
  0.0 414.1 jit_solution(1295653864026888875)
XLA Ops:
  8.5 1.8 convolution_bitcast_fusion
  12.2 1.8 copy.118
  14.1 2.3 copy_dynamic-update-slice_fusion
  16.8 15.9 %dynamic-update-slice.7 = f32[6,4,3,4,3,9,128]{6,5,3,1,0,2,4:T(8,128)} dynamic-update-slice(f32[6,4,3,4,3,9,128]{6,5,3,1,0,2,4:T(8,128)} %copy_dynamic-update-slice_fusion, f32[6,4,3,4,3,1,128]{6,5,3,1,0,2,4:T(1,128)S(1)} %copy.120, s32[]{} %constant.354, s32[]{} %constant.354, s32[]{} %constant.354, s32[]{} %constant.354, s32[]{} %constant.354, s32[]{} %constant.355, s32[]{} %constant.354) | dynamic-update-slice | bytes 884740 | tf_op jit(solution)/shard_map/concatenate | solution.py:45
  32.7 3.8 fusion.70
  36.5 1.7 fusion.4
  40.4 2.2 pad_maximum_fusion.1
  42.6 2.5 copy.121
  59.1 7.7 %collective-permute-start.1 = (bf16[4,8,8,128]{3,2,1,0:T(8,128)(2,1)}, bf16[4,8,8,128]{3,2,1,0:T(8,128)(2,1)}, u32[]{:S(2)}, u32[]{:S(2)}) collective-permute-start(bf16[4,8,8,128]{3,2,1,0:T(8,128)(2,1)} %slice.526), channel_id=1, source_target_pairs={{8,0},{16,8},{24,16},{32,24},{40,32},{48,40},{56,48},{64,56},{72,6... | collective-permute-start | bytes 196616 | tf_op jit(solution)/shard_map/ppermute | solution.py:23
  66.8 2.1 copy.186
  72.1 2.1 collective-permute-start
  87.9 1.8 scatter_fusion.1
  91.8 2.4 scatter_fusion.2
  94.2 2.3 copy.126
  108.2 2.2 gather_fusion.6
  110.4 1.6 fusion.27
  115.8 2.1 gather_fusion.7
  127.6 2.1 gather_fusion.1
  139.8 4.0 convolution_bitcast_fusion.1
  146.0 3.8 scatter-add.66
  149.8 3.8 scatter-add.67
  156.0 2.4 fusion.16
  159.0 245.4 %all-reduce.14.cloned.1.call-done = f32[3,3,3,128,128]{4,3,2,1,0:T(8,128)} async-done(((f32[3,3,3,128,128]{4,3,2,1,0:T(8,128)}), f32[3,3,3,128,128]{4,3,2,1,0:T(8,128)}) %all-reduce.14.cloned.1.call-update) | async-done | bytes 1769488 | tf_op jit(solution)/shard_map/psum | solution.py:171
  404.4 2.9 broadcast_multiply_fusion
  (206 shorter events, 78.5 us)
Async XLA Ops:
  7.2 397.2 %all-reduce.14.cloned.1.call-start = ((), (), s32[]{:S(2)}) async-start(), calls=%async_computation | async-start | bytes 3538944 | tf_op jit(solution)/shard_map/psum | solution.py:171
  8.5 1.8 copy-start.20
  39.3 16.9 %copy-start.19 = (s32[6,3]{0,1:T(4,128)}, s32[6,3]{0,1:T(4,128)S(1)}, u32[]{:S(2)}) copy-start(s32[6,3]{0,1:T(4,128)S(1)} %get-tuple-element.88) | copy-start | bytes 220
  40.2 13.6 %copy-start.29 = (pred[6]{0:T(512)(128)(4,1)}, pred[6]{0:T(512)(128)(4,1)S(1)}, u32[]{:S(2)}) copy-start(pred[6]{0:T(512)(128)(4,1)S(1)} %reduce_or.75) | copy-start | bytes 22
  51.2 2.1 copy-start.23
  51.3 3.9 copy-start.30
  52.4 17.5 %copy-start.24 = (pred[6]{0:T(512)(128)(4,1)}, pred[6]{0:T(512)(128)(4,1)S(1)}, u32[]{:S(2)}) copy-start(pred[6]{0:T(512)(128)(4,1)S(1)} %reduce_or.74) | copy-start | bytes 22
  52.5 17.4 %copy-start.31 = (s32[6]{0:T(128)}, s32[6]{0:T(128)S(1)}, u32[]{:S(2)}) copy-start(s32[6]{0:T(128)S(1)} %select_reduce_fusion.4) | copy-start | bytes 76
  59.1 84.8 %collective-permute-start.1 = (bf16[4,8,8,128]{3,2,1,0:T(8,128)(2,1)}, bf16[4,8,8,128]{3,2,1,0:T(8,128)(2,1)}, u32[]{:S(2)}, u32[]{:S(2)}) collective-permute-start(bf16[4,8,8,128]{3,2,1,0:T(8,128)(2,1)} %slice.526), channel_id=1, source_target_pairs={{8,0},{16,8},{24,16},{32,24},{40,32},{48,40},{56,48},{64,56},{72,6... | collective-permute-start | bytes 196616 | tf_op jit(solution)/shard_map/ppermute | solution.py:23
  71.4 3.5 copy-start.5
  72.1 50.2 %collective-permute-start = (bf16[4,8,8,128]{3,0,2,1:T(4,128)(2,1)}, bf16[4,8,8,128]{3,0,2,1:T(4,128)(2,1)}, u32[]{:S(2)}, u32[]{:S(2)}) collective-permute-start(bf16[4,8,8,128]{3,0,2,1:T(4,128)(2,1)} %copy.94), channel_id=1, source_target_pairs={{0,8},{8,16},{16,24},{24,32},{32,40},{40,48},{48,56},{56,64},{64,7... | collective-permute-start | bytes 196616 | tf_op jit(solution)/shard_map/ppermute | solution.py:23
  77.0 2.3 copy-start.25
  77.0 6.0 %copy-start.33 = (s32[6,1]{0,1:T(1,128)S(1)}, s32[6,1]{0,1:T(1,128)}, u32[]{:S(2)}) copy-start(s32[6,1]{0,1:T(1,128)} %get-tuple-element.51) | copy-start | bytes 76
  77.0 7.1 %copy-start.3 = (bf16[1,6,8,8,8,128]{5,1,4,3,2,0:T(8,128)(2,1)S(1)}, bf16[1,6,8,8,8,128]{5,1,4,3,2,0:T(8,128)(2,1)}, u32[]{:S(2)}) copy-start(bf16[1,6,8,8,8,128]{5,1,4,3,2,0:T(8,128)(2,1)} %copy-done.2) | copy-start | bytes 2359300
  89.7 2.1 copy-start.26
  94.2 12.5 %copy-start.40 = (s32[6]{0:T(128)S(1)}, s32[6]{0:T(128)}, u32[]{:S(2)}) copy-start(s32[6]{0:T(128)} %get-tuple-element.66) | copy-start | bytes 76
  118.8 2.6 copy-start.16
  118.9 3.4 copy-start.32
  133.5 2.3 copy-start.8
  133.5 2.3 copy-start.9
  137.4 2.4 copy-start.18
  137.4 2.4 copy-start.21
  153.6 2.0 copy-start.13
  153.6 2.3 copy-start.15
  (21 other events, 24.9 us)
Sparse Core Ops, SparseCore 0:
  143.9 260.3 all-reduce.13
where the time goes:
time: 416 us; the launch traced here: 414 us
  waiting for transfers between devices  245 us (59%)
  local copies, waits for them, and re-layouts  77.7 us (19%)
  other arithmetic  58.1 us (14%)
  between operations  14.9 us (4%)
  starting transfers between devices  9.9 us (2%)
  matrix products  8.18 us (2%)
    psum x1, waiting for transfers between devices, per_device(): summed = lax.psum(local_grad, ('region', 'group'))  245 us
    concatenate x1, local copies, waits for them, and re-layouts, fold_back(): jnp.concatenate([merged, lax.slice_in_dim(even_rows, 4, 5, 1, which_axis)...  15.9 us
    unnamed x90, local copies, waits for them, and re-layouts  14.1 us
    gather x8, local copies, waits for them, and re-layouts, pick_rows(): gathered = jnp.take(lookup_table, safe_rows, axis=0)  11 us
    ppermute x2, starting transfers between devices, shifted(): return lax.ppermute(block, axis, route)  9.86 us
  transfers between devices with their start and end apart: 3, of which 1 were waited for; matrix products, arithmetic and copies ran while one was open for 21% of the time, Pallas kernels for 0%

commit v1 on v0

--- a/solution.py
+++ b/solution.py
@@ -168,7 +168,7 @@
         jnp.float32
     )
     own_grad = own_grad.at[:, 7].add(pick_rows(returned, (cell_index, in_top)))
-    summed = lax.psum(local_grad, ("region", "group"))
+    summed = lax.psum(lax.psum(local_grad, "region"), "group")
     grad_scale = 1.0 / math.sqrt(
         lax.axis_size("group") * lax.axis_size("region") * block_count * upstream.shape[1] ** 3
     )

time: 416 us -> 340 us (0.82)
  waiting for transfers between devices: 245 us -> 174 us
  other arithmetic: 58.1 us -> 51.1 us
    psum x1 -> x2, waiting for transfers between devices: 245 us -> 174 us  [per_device(): summed = lax.psum(lax.psum(local_grad, 'region'), 'group')]
    unnamed x90 -> x110, local copies, waits for them, and re-layouts: 14.1 us -> 16.4 us
  transfers between devices with their start and end apart: 3 -> 4, of which waited for: 1 -> 2; matrix products, arithmetic and copies ran while one was open for 21% -> 30% of each run, Pallas kernels for 0% -> 0%
where the time goes in v1:
time: 340 us; the launch traced here: 339 us
  waiting for transfers between devices  174 us (51%)
  local copies, waits for them, and re-layouts  81.1 us (24%)
  other arithmetic  51.1 us (15%)
  between operations  15 us (4%)
  starting transfers between devices  10.2 us (3%)
  matrix products  7.31 us (2%)
    psum x2, waiting for transfers between devices, per_device(): summed = lax.psum(lax.psum(local_grad, 'region'), 'group')  174 us
    unnamed x110, local copies, waits for them, and re-layouts  16.4 us
    concatenate x1, local copies, waits for them, and re-layouts, fold_back(): jnp.concatenate([merged, lax.slice_in_dim(even_rows, 4, 5, 1, which_axis)...  15.9 us
    ppermute x2, starting transfers between devices, shifted(): return lax.ppermute(block, axis, route)  9.91 us
    gather x8, local copies, waits for them, and re-layouts, pick_rows(): gathered = jnp.take(lookup_table, safe_rows, axis=0)  9.69 us
    another operation x6, other arithmetic, fold_back(): jnp.stack([lax.slice_in_dim(even_rows, 0, 4, 1, which_axis), middle_part]...  8.46 us
    another operation x3, local copies, waits for them, and re-layouts, fold_back(): jnp.stack([lax.slice_in_dim(even_rows, 0, 4, 1, which_axis), middle_part]...  8.18 us
  transfers between devices with their start and end apart: 4, of which 2 were waited for; matrix products, arithmetic and copies ran while one was open for 30% of the time, Pallas kernels for 0%

profile of v1, /device:TPU:2, one launch (start us, length us, event | category | flops | bytes accessed | tf_op | source)
XLA Modules:
  0.0 338.8 jit_solution(14078835009861905952)
XLA Ops:
  9.1 2.1 copy.186
  12.7 3.8 %collective-permute-start = (bf16[4,8,8,128]{3,0,2,1:T(4,128)(2,1)}, bf16[4,8,8,128]{3,0,2,1:T(4,128)(2,1)}, u32[]{:S(2)}, u32[]{:S(2)}) collective-permute-start(bf16[4,8,8,128]{3,0,2,1:T(4,128)(2,1)} %copy.94), channel_id=1, source_target_pairs={{0,8},{8,16},{16,24},{24,32},{32,40},{40,48},{48,56},{56,64},{64,7... | collective-permute-start | bytes 196616 | tf_op jit(solution)/shard_map/ppermute | solution.py:23
  17.5 2.1 slice_bitcast_fusion.2
  19.6 1.7 fusion.2
  30.2 2.9 pad_maximum_fusion
  33.1 1.8 copy.118
  34.9 2.4 copy_dynamic-update-slice_fusion
  37.8 15.9 %dynamic-update-slice.7 = f32[6,4,3,4,3,9,128]{6,5,3,1,0,2,4:T(8,128)} dynamic-update-slice(f32[6,4,3,4,3,9,128]{6,5,3,1,0,2,4:T(8,128)} %copy_dynamic-update-slice_fusion, f32[6,4,3,4,3,1,128]{6,5,3,1,0,2,4:T(1,128)S(1)} %copy.120, s32[]{} %constant.354, s32[]{} %constant.354, s32[]{} %constant.354, s32[]{} %constant.354, s32[]{} %constant.354, s32[]{} %constant.355, s32[]{} %constant.354) | dynamic-update-slice | bytes 884740 | tf_op jit(solution)/shard_map/concatenate | solution.py:45
  53.7 6.4 %fusion.70 = (f32[6,4,3,4,1,9,128]{6,5,3,1,0,2,4:T(8,128)}, f32[6,4,3,4,9,128]{5,4,3,1,0,2:T(8,128)S(1)}, f32[6,4,3,4,9,128]{5,4,3,1,0,2:T(8,128)}) fusion(f32[6,4,3,4,3,9,128]{6,5,3,1,0,2,4:T(8,128)} %dynamic-update-slice.7), kind=kLoop, calls=%fused_computation.249 | loop fusion | bytes 7962624 | tf_op jit(solution)/shard_map/slice | solution.py:33
  71.3 2.1 gather_fusion.7
  79.1 3.0 pad_maximum_fusion.1
  88.5 2.2 gather_fusion.1
  101.2 4.0 %convolution_bitcast_fusion.1 = f32[3,3,3,128,128]{4,3,2,1,0:T(8,128)} fusion(bf16[6,4,3,4,3,4,1,128]{7,0,6,4,2,5,3,1:T(8,128)(2,1)S(1)} %get-tuple-element.76, bf16[6,4,3,4,3,4,1,128]{7,0,6,4,2,5,3,1:T(8,128)(2,1)S(1)} %get-tuple-element.77, bf16[6,4,3,4,3,4,1,128]{7,0,6,4,2,5,3,1:T(8,128)(2,1)S(1)} %get-tuple-element.75, ...), kind=kOutput, calls=%fused_computation.57 | convolution fusion | flops 342441984 | bytes 4521990 | tf_op jit(solution)/shard_map/nxaybzcf,nxyzo->abcfo/dot_general | solution.py:156
  105.6 4.8 %copy.121 = f32[6,4,3,4,2,9,128]{6,4,3,5,2,1,0:T(2,128)S(1)} copy(f32[6,4,3,4,2,9,128]{6,5,3,1,0,2,4:T(8,128)} %pad_maximum_fusion.1) | data formatting | bytes 5308416 | tf_op jit(solution)/shard_map/stack | solution.py:39
  119.8 6.1 %collective-permute-start.1 = (bf16[4,8,8,128]{3,2,1,0:T(8,128)(2,1)S(1)}, bf16[4,8,8,128]{3,2,1,0:T(8,128)(2,1)S(1)}, u32[]{:S(2)}, u32[]{:S(2)}) collective-permute-start(bf16[4,8,8,128]{3,2,1,0:T(8,128)(2,1)S(1)} %slice.526), channel_id=1, source_target_pairs={{8,0},{16,8},{24,16},{32,24},{40,32},{48,40},{56,48},{64,56},{72,6... | collective-permute-start | bytes 196616 | tf_op jit(solution)/shard_map/ppermute | solution.py:23
  125.9 2.2 copy.124
  134.4 2.3 scatter_fusion.2
  136.7 2.3 copy.126
  141.5 116.9 %all-reduce.15.cloned.1.call-done = f32[3,3,3,128,128]{4,3,2,1,0:T(8,128)} async-done(((f32[3,3,3,128,128]{4,3,2,1,0:T(8,128)}), f32[3,3,3,128,128]{4,3,2,1,0:T(8,128)}) %all-reduce.15.cloned.1.call-update) | async-done | bytes 1769488 | tf_op jit(solution)/shard_map/psum | solution.py:171
  259.0 3.8 %scatter-add.66 = f32[6,8,8,8,128]{4,1,3,2,0:T(8,128)S(1)} dynamic-update-slice(f32[6,8,8,8,128]{4,1,3,2,0:T(8,128)S(1)} %scatter_fusion.3, f32[6,1,8,8,128]{4,1,3,2,0:T(1,128)S(1)} %get-tuple-element.46, s32[]{:T(128)} %constant.164.clone.1, s32[]{:T(128)} %constant.180.clone.1, s32[]{:T(128)} %constant.164.clone.1, s32[]{:T(128)} %constant.164.clone.1, s32[]{:T(128)} %constant.164.clone.1) | dynamic-update-slice | bytes 393220 | tf_op jit(solution)/shard_map/scatter-add | solution.py:166
  262.8 3.8 %scatter-add.67 = f32[6,8,8,8,128]{4,1,3,2,0:T(8,128)S(1)} dynamic-update-slice(f32[6,8,8,8,128]{4,1,3,2,0:T(8,128)S(1)} %scatter-add.66, f32[6,1,8,8,128]{4,1,3,2,0:T(1,128)S(1)} %get-tuple-element.45, s32[]{:T(128)} %constant.164.clone.1, s32[]{:T(128)} %constant.180.clone.1, s32[]{:T(128)} %constant.164.clone.1, s32[]{:T(128)} %constant.164.clone.1, s32[]{:T(128)} %constant.164.clone.1) | dynamic-update-slice | bytes 393220 | tf_op jit(solution)/shard_map/scatter-add | solution.py:170
  268.9 2.4 fusion.16
  271.9 57.1 %all-reduce.17.cloned.1.call-done = f32[3,3,3,128,128]{4,3,2,1,0:T(8,128)} async-done(((f32[3,3,3,128,128]{4,3,2,1,0:T(8,128)}), f32[3,3,3,128,128]{4,3,2,1,0:T(8,128)}) %all-reduce.17.cloned.1.call-update) | async-done | bytes 1769488 | tf_op jit(solution)/shard_map/psum | solution.py:171
  329.1 2.9 broadcast_multiply_fusion
  (229 shorter events, 68.7 us)
Async XLA Ops:
  7.2 9.4 %copy-start = (bf16[3,3,3,128,128]{4,3,2,1,0:T(8,128)(2,1)S(1)}, bf16[3,3,3,128,128]{4,3,2,1,0:T(8,128)(2,1)}, u32[]{:S(2)}) copy-start(bf16[3,3,3,128,128]{4,3,2,1,0:T(8,128)(2,1)} %param.22) | copy-start | bytes 2654212
  7.2 9.4 %copy-start.18 = (bf16[1,6,4,4,4,128]{5,4,3,2,1,0:T(4,128)(2,1)S(1)}, bf16[1,6,4,4,4,128]{5,4,3,2,1,0:T(4,128)(2,1)}, u32[]{:S(2)}) copy-start(bf16[1,6,4,4,4,128]{5,4,3,2,1,0:T(4,128)(2,1)} %param.21) | copy-start | bytes 294916
  7.2 251.2 %all-reduce.15.cloned.1.call-start = ((), (), s32[]{:S(2)}) async-start(), calls=%async_computation | async-start | bytes 3538944 | tf_op jit(solution)/shard_map/psum | solution.py:171
  8.6 8.9 %copy-start.24 = (pred[6]{0:T(512)(128)(4,1)}, pred[6]{0:T(512)(128)(4,1)S(1)}, u32[]{:S(2)}) copy-start(pred[6]{0:T(512)(128)(4,1)S(1)} %get-tuple-element.84) | copy-start | bytes 22
  11.2 18.9 %copy-start.5 = (bf16[1,6,8,8,8,128]{5,1,4,3,2,0:T(8,128)(2,1)}, bf16[1,6,8,8,8,128]{5,1,4,3,2,0:T(8,128)(2,1)S(1)}, u32[]{:S(2)}) copy-start(bf16[1,6,8,8,8,128]{5,1,4,3,2,0:T(8,128)(2,1)S(1)} %copy.186) | copy-start | bytes 2359300
  12.7 70.0 %collective-permute-start = (bf16[4,8,8,128]{3,0,2,1:T(4,128)(2,1)}, bf16[4,8,8,128]{3,0,2,1:T(4,128)(2,1)}, u32[]{:S(2)}, u32[]{:S(2)}) collective-permute-start(bf16[4,8,8,128]{3,0,2,1:T(4,128)(2,1)} %copy.94), channel_id=1, source_target_pairs={{0,8},{8,16},{16,24},{24,32},{32,40},{40,48},{48,56},{56,64},{64,7... | collective-permute-start | bytes 196616 | tf_op jit(solution)/shard_map/ppermute | solution.py:23
  22.5 7.6 %copy-start.33 = (pred[6]{0:T(512)(128)(4,1)}, pred[6]{0:T(512)(128)(4,1)S(1)}, u32[]{:S(2)}) copy-start(pred[6]{0:T(512)(128)(4,1)S(1)} %reduce_or.75) | copy-start | bytes 22
  25.9 47.6 %copy-start.27 = (pred[6]{0:T(512)(128)(4,1)}, pred[6]{0:T(512)(128)(4,1)S(1)}, u32[]{:S(2)}) copy-start(pred[6]{0:T(512)(128)(4,1)S(1)} %reduce_or.79) | copy-start | bytes 22
  53.7 6.4 %copy-start.51 = (s32[6]{0:T(128)S(1)}, s32[6]{0:T(128)}, u32[]{:S(2)}) copy-start(s32[6]{0:T(128)} %select_reduce_fusion.2) | copy-start | bytes 76
  53.7 7.5 %copy-start.35 = (s32[6]{0:T(128)S(1)}, s32[6]{0:T(128)}, u32[]{:S(2)}) copy-start(s32[6]{0:T(128)} %select_reduce_fusion.5) | copy-start | bytes 76
  53.7 8.2 %copy-start.36 = (s32[6]{0:T(128)S(1)}, s32[6]{0:T(128)}, u32[]{:S(2)}) copy-start(s32[6]{0:T(128)} %select_reduce_fusion.4) | copy-start | bytes 76
  53.7 10.5 %copy-start.46 = (s32[6]{0:T(128)S(1)}, s32[6]{0:T(128)}, u32[]{:S(2)}) copy-start(s32[6]{0:T(128)} %fusion.68) | copy-start | bytes 76
  53.7 11.1 %copy-start.34 = (pred[6]{0:T(512)(128)(4,1)S(1)}, pred[6]{0:T(512)(128)(4,1)}, u32[]{:S(2)}) copy-start(pred[6]{0:T(512)(128)(4,1)} %copy-done.33) | copy-start | bytes 22
  53.7 11.1 %copy-start.39 = (pred[6,1]{0,1:T(4,128)(4,1)S(1)}, pred[6,1]{0,1:T(4,128)(4,1)}, u32[]{:S(2)}) copy-start(pred[6,1]{0,1:T(4,128)(4,1)} %get-tuple-element.103) | copy-start | bytes 22
  53.7 11.7 %copy-start.49 = (s32[6]{0:T(128)S(1)}, s32[6]{0:T(128)}, u32[]{:S(2)}) copy-start(s32[6]{0:T(128)} %get-tuple-element.105) | copy-start | bytes 76
  53.7 12.2 %copy-start.17 = (bf16[6,8,8,128]{3,0,2,1:T(8,128)(2,1)S(1)}, bf16[6,8,8,128]{3,0,2,1:T(8,128)(2,1)}, u32[]{:S(2)}) copy-start(bf16[6,8,8,128]{3,0,2,1:T(8,128)(2,1)} %slice_bitcast_fusion.14) | copy-start | bytes 294916
  53.7 12.9 %copy-start.47 = (s32[6]{0:T(128)S(1)}, s32[6]{0:T(128)}, u32[]{:S(2)}) copy-start(s32[6]{0:T(128)} %get-tuple-element.104) | copy-start | bytes 76
  105.3 223.8 %all-reduce.17.cloned.1.call-start = ((), (), s32[]{:S(2)}) async-start(), calls=%async_computation.1 | async-start | bytes 3538944 | tf_op jit(solution)/shard_map/psum | solution.py:171
  113.4 3.7 %copy-start.23 = (s32[6]{0:T(128)S(1)}, s32[6]{0:T(128)}, u32[]{:S(2)}) copy-start(s32[6]{0:T(128)} %get-tuple-element.54) | copy-start | bytes 76
  113.4 4.6 %copy-start.22 = (s32[6]{0:T(128)S(1)}, s32[6]{0:T(128)}, u32[]{:S(2)}) copy-start(s32[6]{0:T(128)} %get-tuple-element.52) | copy-start | bytes 76
  114.9 4.0 %copy-start.20 = (s32[6]{0:T(128)S(1)}, s32[6]{0:T(128)}, u32[]{:S(2)}) copy-start(s32[6]{0:T(128)} %get-tuple-element.49) | copy-start | bytes 76
  119.8 21.2 %collective-permute-start.1 = (bf16[4,8,8,128]{3,2,1,0:T(8,128)(2,1)S(1)}, bf16[4,8,8,128]{3,2,1,0:T(8,128)(2,1)S(1)}, u32[]{:S(2)}, u32[]{:S(2)}) collective-permute-start(bf16[4,8,8,128]{3,2,1,0:T(8,128)(2,1)S(1)} %slice.526), channel_id=1, source_target_pairs={{8,0},{16,8},{24,16},{32,24},{40,32},{48,40},{56,48},{64,56},{72,6... | collective-permute-start | bytes 196616 | tf_op jit(solution)/shard_map/ppermute | solution.py:23
  139.1 119.4 %copy-start.30 = (pred[6]{0:T(512)(128)(4,1)S(1)}, pred[6]{0:T(512)(128)(4,1)}, u32[]{:S(2)}) copy-start(pred[6]{0:T(512)(128)(4,1)} %get-tuple-element.47) | copy-start | bytes 22
  139.1 119.4 %copy-start.31 = (pred[6]{0:T(512)(128)(4,1)S(1)}, pred[6]{0:T(512)(128)(4,1)}, u32[]{:S(2)}) copy-start(pred[6]{0:T(512)(128)(4,1)} %get-tuple-element.83) | copy-start | bytes 22
  (32 other events, 51.9 us)
Sparse Core Ops, SparseCore 0:
  105.4 153.0 all-reduce.14
  260.9 68.0 all-reduce.16
